TPU v7x, 32 devices: a whole 2x2x4 slice. The times are simulated.
32 devices in a mesh: dp: 4 (over z), expert: 4 (over y, core), loop: 2 (over x).
Axes of the slice: x: 2, y: 2, z: 4, core: 2. Of those that a mesh axis runs over, the one named last changes fastest.
Arguments:
- x_send: bfloat16 [512, 4096], P(('dp', 'expert', 'loop')), may hold values from -6 to 6
- cot_send: bfloat16 [512, 4096], P(('dp', 'expert', 'loop')), may hold values from -6 to 6
- counts: int32 [32, 4], P(('dp', 'expert', 'loop')), may hold values from 0 to 4, as said below
- w_gate: bfloat16 [4, 4096, 768], P('expert', None, 'loop'), may hold values from -0.09375 to 0.09375
- w_up: bfloat16 [4, 4096, 768], P('expert', None, 'loop'), may hold values from -0.09375 to 0.09375
- w_down: bfloat16 [4, 4096, 768], P('expert', None, 'loop'), may hold values from -0.21875 to 0.21875
Outputs:
- grad_rows: bfloat16 [512, 4096], P(('dp', 'expert', 'loop'))
- grad_down: float32 [4, 4096, 768], P('expert', 'dp', 'loop')
Inputs may be any that keep to these rules, and one draw needn't show every extreme that they name: counts[s, e] is how many of the 4 slots of device s for owner e hold rows, filled from slot 0; in each group of 8 consecutive devices one owner, drawn anew, receives 4 rows from every device, and every other owner at most 2 from each device.
All inputs are finite; a program needn't handle non-finite values.
Results may differ from a plain program's by a relative error of at most 0.0095.
Values may be sent and summed in bfloat16 or wider, within the bound.
No kernel may reach another device: no remote copies, remote signals or barrier semaphores. Data moves between devices by JAX's collectives and lax.ppermute only.
A program may use at most 64 MiB of HBM per device.

v0:
```python
import jax
import jax.numpy as jnp
from jax import lax
from jax.sharding import PartitionSpec as P


def local(x_send, cot_send, counts, w_gate, w_up, w_down):
    owner_count = counts.shape[1]
    capacity = x_send.shape[0] // owner_count
    live_slot = (jnp.arange(capacity, dtype=jnp.int32)[None, :] < counts[0][:, None]).reshape(
        owner_count * capacity, 1
    )
    zero_value = jnp.zeros((), jnp.bfloat16)
    inputs = jnp.where(live_slot, x_send, zero_value)
    cotans = jnp.where(live_slot, cot_send, zero_value)
    arrived, arrived_cot = (
        lax.all_to_all(inputs, "expert", split_axis=0, concat_axis=0, tiled=True),
        lax.all_to_all(cotans, "expert", split_axis=0, concat_axis=0, tiled=True),
    )
    gathered, gathered_cot = (
        lax.all_gather(arrived, "loop", axis=0, tiled=True),
        lax.all_gather(arrived_cot, "loop", axis=0, tiled=True),
    )
    gate_local = w_gate[0]
    up_local = w_up[0]
    down_local = w_down[0]
    gate_pre = jnp.dot(gathered, gate_local, preferred_element_type=jnp.float32)
    up_proj = jnp.dot(gathered, up_local, preferred_element_type=jnp.float32)
    sigmoid_gate = jax.nn.sigmoid(gate_pre)
    active = gate_pre * sigmoid_gate
    hidden = (active * up_proj).astype(jnp.bfloat16)
    grad_hidden = jnp.dot(gathered_cot, down_local, preferred_element_type=jnp.float32)
    grad_gate = (
        grad_hidden * up_proj * sigmoid_gate * (1.0 + gate_pre * (1.0 - sigmoid_gate))
    ).astype(jnp.bfloat16)
    grad_upp = (grad_hidden * active).astype(jnp.bfloat16)
    contract_last = (((1,), (1,)), ((), ()))
    contract_first = (((0,), (0,)), ((), ()))
    partial_value = lax.dot_general(
        grad_gate, gate_local, contract_last, preferred_element_type=jnp.float32
    )
    partial_value = partial_value + lax.dot_general(
        grad_upp, up_local, contract_last, preferred_element_type=jnp.float32
    )
    summed = lax.psum_scatter(
        lax.optimization_barrier(partial_value.astype(jnp.bfloat16))
        .astype(jnp.float32)
        .astype(jnp.bfloat16),
        "loop",
        scatter_dimension=0,
        tiled=True,
    )
    grad_rows = lax.all_to_all(summed, "expert", split_axis=0, concat_axis=0, tiled=True)
    column_part = lax.all_to_all(gathered_cot, "dp", split_axis=1, concat_axis=0, tiled=True)
    hidden_all = lax.all_gather(hidden, "dp", axis=0, tiled=True)
    result = lax.dot_general(
        column_part, hidden_all, contract_first, preferred_element_type=jnp.float32
    )
    grad_down = result[None]
    return (grad_rows, grad_down)


def solution(mesh):
    in_specs = (
        P(("dp", "expert", "loop"), None),
        P(("dp", "expert", "loop"), None),
        P(("dp", "expert", "loop"), None),
        P("expert", None, "loop"),
        P("expert", None, "loop"),
        P("expert", None, "loop"),
    )
    out_specs = (P(("dp", "expert", "loop"), None), P("expert", "dp", "loop"))
    return jax.shard_map(local, mesh=mesh, in_specs=in_specs, out_specs=out_specs, check_vma=False)
```

profile of v0, /device:TPU:0, one launch (start us, length us, event | category | flops | bytes accessed | tf_op | source)
XLA Modules:
  0.0 81.4 jit_solution(18439740056307525910)
XLA Ops:
  7.2 0.0 copy-start
  7.2 0.9 %iota_compare_fusion = pred[4,4]{1,0:T(4,128)(4,1)S(1)} fusion(s32[4]{0:T(128)} %bitcast.33), kind=kLoop, calls=%fused_computation.21 | loop fusion | flops 16 | bytes 32 | tf_op jit(solution)/shard_map/lt | solution.py:10
  8.1 0.1 lt.26
  8.1 1.1 %broadcast_select_fusion.1 = (bf16[16,4096]{1,0:T(8,128)(2,1)S(1)}, bf16[16,4096]{1,0:T(8,128)(2,1)S(1)}) fusion(bf16[16,4096]{1,0:T(8,128)(2,1)} %param.7, pred[16]{0:T(512)(128)(4,1)S(1)} %lt.26, bf16[16,4096]{1,0:T(8,128)(2,1)} %param.6), kind=kLoop, calls=%fused_computation.14 | loop fusion | flops 131072 | bytes 524304 | tf_op jit(solution)/shard_map/jit(_where)/select_n | solution.py:15
  9.2 0.7 all_to_all.38
  9.9 4.3 %all-to-all-start = ((bf16[4,4,4096]{2,1,0:T(4,128)(2,1)}), bf16[4,4,4096]{2,1,0:T(4,128)(2,1)S(1)}, u32[]{:S(2)}, u32[]{:S(2)}) async-start(bf16[4,4,4096]{2,1,0:T(4,128)(2,1)} %all_to_all.38), calls=%async_computation | async-start | bytes 262144 | tf_op jit(solution)/shard_map/all_to_all | solution.py:18
  14.2 0.7 all_to_all.41
  14.9 3.9 %all-to-all-done = bf16[4,4,4096]{2,1,0:T(4,128)(2,1)S(1)} async-done(((bf16[4,4,4096]{2,1,0:T(4,128)(2,1)}), bf16[4,4,4096]{2,1,0:T(4,128)(2,1)S(1)}, u32[]{:S(2)}, u32[]{:S(2)}) %all-to-all-start) | async-done | bytes 131104 | tf_op jit(solution)/shard_map/all_to_all | solution.py:18
  18.8 4.0 %all-to-all-start.1 = ((bf16[4,4,4096]{2,1,0:T(4,128)(2,1)}), bf16[4,4,4096]{2,1,0:T(4,128)(2,1)}, u32[]{:S(2)}, u32[]{:S(2)}) async-start(bf16[4,4,4096]{2,1,0:T(4,128)(2,1)} %all_to_all.41), calls=%async_computation.1 | async-start | bytes 262144 | tf_op jit(solution)/shard_map/all_to_all | solution.py:17
  22.7 0.0 reduce-scatter.2.cloned.1.call-start
  22.8 6.7 %all_gather.9 = bf16[32,4096]{1,0:T(8,128)(2,1)S(1)} all-gather(bf16[16,4096]{1,0:T(8,128)(2,1)S(1)} %all_to_all.40), channel_id=1, replica_groups=mesh['dp'=4,'expert'=4,'loop'=2] {'loop'}, dimensions={0}, use_global_device_ids=true | all-gather | bytes 393216 | tf_op jit(solution)/shard_map/all_gather | solution.py:22
  29.6 0.0 all-to-all-done.1
  29.6 0.9 %all_to_all.43 = bf16[16,4096]{1,0:T(8,128)(2,1)S(1)} reshape(bf16[4,4,4096]{2,1,0:T(4,128)(2,1)} %all-to-all-done.1) | data formatting | bytes 262144 | tf_op jit(solution)/shard_map/all_to_all | solution.py:17
  30.5 0.0 copy-start.1
  30.5 6.0 %all_gather.10 = bf16[32,4096]{1,0:T(8,128)(2,1)S(1)} all-gather(bf16[16,4096]{1,0:T(8,128)(2,1)S(1)} %all_to_all.43), channel_id=1, replica_groups=mesh['dp'=4,'expert'=4,'loop'=2] {'loop'}, dimensions={0}, use_global_device_ids=true | all-gather | bytes 393216 | tf_op jit(solution)/shard_map/all_gather | solution.py:21
  36.5 2.4 %fusion.8 = f32[32,384]{1,0:T(8,128)S(1)} fusion(bf16[32,4096]{1,0:T(8,128)(2,1)S(1)} %all_gather.9, bf16[1,4096,384]{2,1,0:T(8,128)(2,1)} %param.11), kind=kOutput, calls=%fused_computation.9 | convolution fusion | flops 100663296 | bytes 3457024 | tf_op jit(solution)/shard_map/dot_general | solution.py:32
  39.0 0.0 copy-done.1
  39.0 0.5 fusion.3
  39.5 0.0 copy-done
  39.5 0.6 multiply_convert_fusion
  40.1 1.1 %fusion.1 = f32[32,4096]{1,0:T(8,128)S(1)} fusion(bf16[1,4096,384]{2,1,0:T(8,128)(2,1)S(1)} %copy-done.1, f32[32,384]{1,0:T(8,128)S(1)} %fusion.3, f32[32,384]{1,0:T(8,128)S(1)} %fusion.8, f32[32,384]{1,0:T(8,128)S(1)} %get-tuple-element.5), kind=kOutput, calls=%fused_computation.2 | convolution fusion | flops 100786176 | bytes 3817472 | tf_op jit(solution)/shard_map/dot_general | solution.py:39
  41.2 1.8 %fusion = bf16[32,4096]{1,0:T(8,128)(2,1)} fusion(f32[32,4096]{1,0:T(8,128)S(1)} %fusion.1, bf16[1,4096,384]{2,1,0:T(8,128)(2,1)S(1)} %copy-done, f32[32,384]{1,0:T(8,128)S(1)} %fusion.8, f32[32,384]{1,0:T(8,128)S(1)} %fusion.3), kind=kOutput, calls=%fused_computation.1 | convolution fusion | flops 100999168 | bytes 4030464 | tf_op jit(solution)/shard_map/dot_general | solution.py:42
  42.9 0.0 reduce-scatter.2.cloned.1.call-update
  43.0 0.7 copy.12
  43.7 4.9 %all-to-all-start.3 = ((bf16[32,4,1024]{2,0,1:T(8,128)(2,1)}), bf16[32,4,1024]{2,0,1:T(8,128)(2,1)S(1)}, u32[]{:S(2)}, u32[]{:S(2)}) async-start(bf16[32,4,1024]{2,0,1:T(8,128)(2,1)} %bitcast.31), calls=%async_computation.4 | async-start | bytes 524288 | tf_op jit(solution)/shard_map/all_to_all | solution.py:54
  48.6 15.7 %all_gather.11 = bf16[128,384]{1,0:T(8,128)(2,1)} all-gather(bf16[32,384]{1,0:T(8,128)(2,1)S(1)} %get-tuple-element.4), channel_id=1, replica_groups=mesh['dp'=4,'expert'=4,'loop'=2] {'dp'}, dimensions={0}, use_global_device_ids=true | all-gather | bytes 122880 | tf_op jit(solution)/shard_map/all_gather | solution.py:55
  64.3 0.0 reduce-scatter.2.cloned.1.call-done
  64.3 1.6 %all_to_all.44 = bf16[4,4,4096]{2,1,0:T(4,128)(2,1)} reshape(bf16[16,4096]{1,0:T(8,128)(2,1)} %reduce-scatter.2.cloned.1.call-done) | data formatting | bytes 262144 | tf_op jit(solution)/shard_map/all_to_all | solution.py:53
  66.0 0.0 all-to-all-done.3
  66.0 3.3 %all-to-all-start.2 = ((bf16[4,4,4096]{2,1,0:T(4,128)(2,1)}), bf16[4,4,4096]{2,1,0:T(4,128)(2,1)S(1)}, u32[]{:S(2)}, u32[]{:S(2)}) async-start(bf16[4,4,4096]{2,1,0:T(4,128)(2,1)} %all_to_all.44), calls=%async_computation.3 | async-start | bytes 262144 | tf_op jit(solution)/shard_map/all_to_all | solution.py:53
  69.3 2.4 %convolution_bitcast_fusion = f32[1,1024,384]{2,1,0:T(8,128)} fusion(bf16[128,1024]{1,0:T(8,128)(2,1)S(1)} %bitcast.32, bf16[128,384]{1,0:T(8,128)(2,1)} %all_gather.11), kind=kOutput, calls=%fused_computation.11 | convolution fusion | flops 100663296 | bytes 1933312 | tf_op jit(solution)/shard_map/dot_general | solution.py:56
  71.7 2.1 %all-to-all-done.2 = bf16[4,4,4096]{2,1,0:T(4,128)(2,1)S(1)} async-done(((bf16[4,4,4096]{2,1,0:T(4,128)(2,1)}), bf16[4,4,4096]{2,1,0:T(4,128)(2,1)S(1)}, u32[]{:S(2)}, u32[]{:S(2)}) %all-to-all-start.2) | async-done | bytes 131104 | tf_op jit(solution)/shard_map/all_to_all | solution.py:53
  73.9 0.7 all_to_all.46
  (1 shorter events, 0.0 us)
Async XLA Ops:
  7.2 32.4 %copy-start = (bf16[1,4096,384]{2,1,0:T(8,128)(2,1)S(1)}, bf16[1,4096,384]{2,1,0:T(8,128)(2,1)}, u32[]{:S(2)}) copy-start(bf16[1,4096,384]{2,1,0:T(8,128)(2,1)} %param.10) | copy-start | bytes 9437188
  9.9 8.9 %all-to-all-start = ((bf16[4,4,4096]{2,1,0:T(4,128)(2,1)}), bf16[4,4,4096]{2,1,0:T(4,128)(2,1)S(1)}, u32[]{:S(2)}, u32[]{:S(2)}) async-start(bf16[4,4,4096]{2,1,0:T(4,128)(2,1)} %all_to_all.38), calls=%async_computation | async-start | bytes 262144 | tf_op jit(solution)/shard_map/all_to_all | solution.py:18
  18.8 10.8 %all-to-all-start.1 = ((bf16[4,4,4096]{2,1,0:T(4,128)(2,1)}), bf16[4,4,4096]{2,1,0:T(4,128)(2,1)}, u32[]{:S(2)}, u32[]{:S(2)}) async-start(bf16[4,4,4096]{2,1,0:T(4,128)(2,1)} %all_to_all.41), calls=%async_computation.1 | async-start | bytes 262144 | tf_op jit(solution)/shard_map/all_to_all | solution.py:17
  22.7 41.6 %reduce-scatter.2.cloned.1.call-start = ((), (), s32[]{:S(2)}) async-start(), calls=%async_computation.5 | async-start | bytes 393216 | tf_op jit(solution)/shard_map/reduce_scatter | solution.py:45
  30.5 8.4 %copy-start.1 = (bf16[1,4096,384]{2,1,0:T(8,128)(2,1)S(1)}, bf16[1,4096,384]{2,1,0:T(8,128)(2,1)}, u32[]{:S(2)}) copy-start(bf16[1,4096,384]{2,1,0:T(8,128)(2,1)} %param.9) | copy-start | bytes 9437188
  43.7 22.3 %all-to-all-start.3 = ((bf16[32,4,1024]{2,0,1:T(8,128)(2,1)}), bf16[32,4,1024]{2,0,1:T(8,128)(2,1)S(1)}, u32[]{:S(2)}, u32[]{:S(2)}) async-start(bf16[32,4,1024]{2,0,1:T(8,128)(2,1)} %bitcast.31), calls=%async_computation.4 | async-start | bytes 524288 | tf_op jit(solution)/shard_map/all_to_all | solution.py:54
  66.0 7.9 %all-to-all-start.2 = ((bf16[4,4,4096]{2,1,0:T(4,128)(2,1)}), bf16[4,4,4096]{2,1,0:T(4,128)(2,1)S(1)}, u32[]{:S(2)}, u32[]{:S(2)}) async-start(bf16[4,4,4096]{2,1,0:T(4,128)(2,1)} %all_to_all.44), calls=%async_computation.3 | async-start | bytes 262144 | tf_op jit(solution)/shard_map/all_to_all | solution.py:53
Sparse Core Ops, SparseCore 0:
  43.1 13.1 reduce-scatter.1
where the time goes:
time: 82 us; the launch traced here: 81.4 us
  blocking collectives  28.5 us (35%)
  starting transfers between devices  16.5 us (20%)
  between operations  14.1 us (17%)
  matrix products  8.8 us (11%)
  waiting for transfers between devices  6.05 us (7%)
  local copies, waits for them, and re-layouts  5.53 us (7%)
  other arithmetic  1.94 us (2%)
    all_gather x1, blocking collectives, local(): hidden_all = lax.all_gather(hidden, 'dp', axis=0, tiled=True)  15.7 us
    all_gather x1, blocking collectives, local(): lax.all_gather(arrived_cot, 'loop', axis=0, tiled=True)  6.73 us
    all_gather x1, blocking collectives, local(): lax.all_gather(arrived, 'loop', axis=0, tiled=True)  6 us
    all_to_all x1, starting transfers between devices, local(): lax.all_to_all(gathered_cot, 'dp', split_axis=1, concat_axis=0, tiled=True)  4.9 us
    all_to_all x1, starting transfers between devices, local(): lax.all_to_all(cotans, 'expert', split_axis=0, concat_axis=0, tiled=True)  4.26 us
    all_to_all x1, starting transfers between devices, local(): lax.all_to_all(inputs, 'expert', split_axis=0, concat_axis=0, tiled=True)  3.95 us
    all_to_all x1, waiting for transfers between devices, local(): lax.all_to_all(cotans, 'expert', split_axis=0, concat_axis=0, tiled=True)  3.89 us
    all_to_all x1, starting transfers between devices, local(): lax.all_to_all(summed, 'expert', split_axis=0, concat_axis=0, tiled=True)  3.33 us
  transfers between devices with their start and end apart: 5, of which 2 were waited for; matrix products, arithmetic and copies ran while one was open for 4% of the time, Pallas kernels for 0%

commit v1 on v0

--- a/solution.py
+++ b/solution.py
@@ -17,8 +17,22 @@
         lax.all_to_all(inputs, "expert", split_axis=0, concat_axis=0, tiled=True),
         lax.all_to_all(cotans, "expert", split_axis=0, concat_axis=0, tiled=True),
     )
+
+    def views_mark(incoming_x):
+        u_next, s_next = (lax.axis_size("loop"), lax.axis_index("loop"))
+        block_out, a_next = (incoming_x, 1)
+        while a_next < u_next:
+            g_now = lax.ppermute(
+                block_out, "loop", list(map(lambda pp: (pp, pp ^ a_next), range(u_next)))
+            )
+            t_next = jnp.concatenate([block_out, g_now], 0)
+            long_array = jnp.concatenate([g_now, block_out], 0)
+            block_out = jnp.where(s_next & a_next == 0, t_next, long_array)
+            a_next = 2 * a_next
+        return block_out
+
     gathered, gathered_cot = (
-        lax.all_gather(arrived, "loop", axis=0, tiled=True),
+        views_mark(arrived),
         lax.all_gather(arrived_cot, "loop", axis=0, tiled=True),
     )
     gate_local = w_gate[0]

time: 82 us -> 79.5 us (0.970)
  blocking collectives: 28.5 us -> 22.5 us
  starting transfers between devices: 16.5 us -> 18.3 us
  waiting for transfers between devices: 6.05 us -> 7.07 us
    all_gather x1 -> x0, blocking collectives: 6 us -> none  [local(): lax.all_gather(arrived, 'loop', axis=0, tiled=True)]
    ppermute x0 -> x1, starting transfers between devices: none -> 1.81 us  [views_mark(): lax.ppermute(block_out, 'loop', list(map(lambda pp: (pp, pp ^ a_next), ra...]
    ppermute x0 -> x1, waiting for transfers between devices: none -> 1.02 us  [views_mark(): lax.ppermute(block_out, 'loop', list(map(lambda pp: (pp, pp ^ a_next), ra...]
  transfers between devices with their start and end apart: 5 -> 6, of which waited for: 2 -> 3; matrix products, arithmetic and copies ran while one was open for 4% -> 7% of each run, Pallas kernels for 0% -> 0%
where the time goes in v1:
time: 79.5 us; the launch traced here: 78.9 us
  blocking collectives  22.5 us (28%)
  starting transfers between devices  18.3 us (23%)
  between operations  14.1 us (18%)
  matrix products  9.45 us (12%)
  waiting for transfers between devices  7.07 us (9%)
  local copies, waits for them, and re-layouts  5.54 us (7%)
  other arithmetic  1.94 us (2%)
    all_gather x1, blocking collectives, local(): hidden_all = lax.all_gather(hidden, 'dp', axis=0, tiled=True)  15.7 us
    all_gather x1, blocking collectives, local(): lax.all_gather(arrived_cot, 'loop', axis=0, tiled=True)  6.72 us
    all_to_all x1, starting transfers between devices, local(): lax.all_to_all(gathered_cot, 'dp', split_axis=1, concat_axis=0, tiled=True)  4.9 us
    all_to_all x1, starting transfers between devices, local(): lax.all_to_all(cotans, 'expert', split_axis=0, concat_axis=0, tiled=True)  4.26 us
    all_to_all x1, starting transfers between devices, local(): lax.all_to_all(inputs, 'expert', split_axis=0, concat_axis=0, tiled=True)  3.95 us
    all_to_all x1, waiting for transfers between devices, local(): lax.all_to_all(cotans, 'expert', split_axis=0, concat_axis=0, tiled=True)  3.89 us
    all_to_all x1, starting transfers between devices, local(): lax.all_to_all(summed, 'expert', split_axis=0, concat_axis=0, tiled=True)  3.33 us
    dot_general x1, matrix products, local(): lax.dot_general(column_part, hidden_all, contract_first, preferred_elemen...  2.43 us
  transfers between devices with their start and end apart: 6, of which 3 were waited for; matrix products, arithmetic and copies ran while one was open for 7% of the time, Pallas kernels for 0%

profile of v1, /device:TPU:0, one launch (start us, length us, event | category | flops | bytes accessed | tf_op | source)
XLA Modules:
  0.0 78.9 jit_solution(11130968878800677489)
XLA Ops:
  7.2 0.0 copy-start
  7.2 0.9 %iota_compare_fusion = pred[4,4]{1,0:T(4,128)(4,1)S(1)} fusion(s32[4]{0:T(128)} %bitcast.31), kind=kLoop, calls=%fused_computation.22 | loop fusion | flops 16 | bytes 32 | tf_op jit(solution)/shard_map/lt | solution.py:10
  8.1 0.1 lt.26
  8.1 1.1 %broadcast_select_fusion.1 = (bf16[16,4096]{1,0:T(8,128)(2,1)S(1)}, bf16[16,4096]{1,0:T(8,128)(2,1)S(1)}) fusion(bf16[16,4096]{1,0:T(8,128)(2,1)} %param.7, pred[16]{0:T(512)(128)(4,1)S(1)} %lt.26, bf16[16,4096]{1,0:T(8,128)(2,1)} %param.6), kind=kLoop, calls=%fused_computation.15 | loop fusion | flops 131072 | bytes 524304 | tf_op jit(solution)/shard_map/jit(_where)/select_n | solution.py:15
  9.2 0.7 all_to_all.38
  9.9 4.3 %all-to-all-start = ((bf16[4,4,4096]{2,1,0:T(4,128)(2,1)}), bf16[4,4,4096]{2,1,0:T(4,128)(2,1)S(1)}, u32[]{:S(2)}, u32[]{:S(2)}) async-start(bf16[4,4,4096]{2,1,0:T(4,128)(2,1)} %all_to_all.38), calls=%async_computation | async-start | bytes 262144 | tf_op jit(solution)/shard_map/all_to_all | solution.py:18
  14.2 0.7 all_to_all.41
  14.9 3.9 %all-to-all-done = bf16[4,4,4096]{2,1,0:T(4,128)(2,1)S(1)} async-done(((bf16[4,4,4096]{2,1,0:T(4,128)(2,1)}), bf16[4,4,4096]{2,1,0:T(4,128)(2,1)S(1)}, u32[]{:S(2)}, u32[]{:S(2)}) %all-to-all-start) | async-done | bytes 131104 | tf_op jit(solution)/shard_map/all_to_all | solution.py:18
  18.8 3.9 %all-to-all-start.1 = ((bf16[4,4,4096]{2,1,0:T(4,128)(2,1)}), bf16[4,4,4096]{2,1,0:T(4,128)(2,1)}, u32[]{:S(2)}, u32[]{:S(2)}) async-start(bf16[4,4,4096]{2,1,0:T(4,128)(2,1)} %all_to_all.41), calls=%async_computation.1 | async-start | bytes 262144 | tf_op jit(solution)/shard_map/all_to_all | solution.py:17
  22.7 0.0 reduce-scatter.2.cloned.1.call-start
  22.8 6.7 %all_gather.6 = bf16[32,4096]{1,0:T(8,128)(2,1)S(1)} all-gather(bf16[16,4096]{1,0:T(8,128)(2,1)S(1)} %all_to_all.40), channel_id=1, replica_groups=mesh['dp'=4,'expert'=4,'loop'=2] {'loop'}, dimensions={0}, use_global_device_ids=true | all-gather | bytes 393216 | tf_op jit(solution)/shard_map/all_gather | solution.py:36
  29.6 0.0 all-to-all-done.1
  29.6 0.9 %all_to_all.43 = bf16[16,4096]{1,0:T(8,128)(2,1)S(1)} reshape(bf16[4,4,4096]{2,1,0:T(4,128)(2,1)} %all-to-all-done.1) | data formatting | bytes 262144 | tf_op jit(solution)/shard_map/all_to_all | solution.py:17
  30.5 0.0 copy-start.1
  30.5 1.8 %collective-permute-start = (bf16[16,4096]{1,0:T(8,128)(2,1)S(1)}, bf16[16,4096]{1,0:T(8,128)(2,1)S(1)}, u32[]{:S(2)}, u32[]{:S(2)}) collective-permute-start(bf16[16,4096]{1,0:T(8,128)(2,1)S(1)} %all_to_all.43), channel_id=1, source_target_pairs={{0,1},{1,0},{2,3},{3,2},{4,5},{5,4},{6,7},{7,6},{8,9},{9,8},{10,11... | collective-permute-start | bytes 393224 | tf_op jit(solution)/shard_map/ppermute | solution.py:25
  32.3 2.4 %fusion.8 = f32[32,384]{1,0:T(8,128)S(1)} fusion(bf16[32,4096]{1,0:T(8,128)(2,1)S(1)} %all_gather.6, bf16[1,4096,384]{2,1,0:T(8,128)(2,1)} %param.11), kind=kOutput, calls=%fused_computation.9 | convolution fusion | flops 100663296 | bytes 3457024 | tf_op jit(solution)/shard_map/dot_general | solution.py:46
  34.8 1.0 %collective-permute-done = bf16[16,4096]{1,0:T(8,128)(2,1)S(1)} collective-permute-done((bf16[16,4096]{1,0:T(8,128)(2,1)S(1)}, bf16[16,4096]{1,0:T(8,128)(2,1)S(1)}, u32[]{:S(2)}, u32[]{:S(2)}) %collective-permute-start) | collective-permute-done | bytes 131104 | tf_op jit(solution)/shard_map/ppermute | solution.py:25
  35.8 0.0 copy-done.1
  35.8 0.6 fusion.3
  36.4 0.0 copy-done
  36.4 1.2 %multiply_convert_fusion = (bf16[32,384]{1,0:T(8,128)(2,1)}, f32[32,384]{1,0:T(8,128)S(1)}) fusion(f32[32,384]{1,0:T(8,128)S(1)} %fusion.3, bf16[1,4096,384]{2,1,0:T(8,128)(2,1)S(1)} %copy-done, bf16[16,4096]{1,0:T(8,128)(2,1)S(1)} %collective-permute-done, bf16[16,4096]{1,0:T(8,128)(2,1)S(1)} %all_to_all.43, pred[]{:T(512)S(6)} %eq.3), kind=kOutput, calls=%fused_computation.16 | convolution fusion | flops 101916672 | bytes 3530753 | tf_op jit(solution)/shard_map/dot_general | solution.py:42
  37.6 1.1 %fusion.1 = f32[32,4096]{1,0:T(8,128)S(1)} fusion(bf16[1,4096,384]{2,1,0:T(8,128)(2,1)S(1)} %copy-done.1, f32[32,384]{1,0:T(8,128)S(1)} %fusion.3, f32[32,384]{1,0:T(8,128)S(1)} %fusion.8, f32[32,384]{1,0:T(8,128)S(1)} %get-tuple-element.5), kind=kOutput, calls=%fused_computation.2 | convolution fusion | flops 100786176 | bytes 3817472 | tf_op jit(solution)/shard_map/dot_general | solution.py:53
  38.6 0.0 copy-start.2
  38.6 1.8 %fusion = bf16[32,4096]{1,0:T(8,128)(2,1)} fusion(f32[32,4096]{1,0:T(8,128)S(1)} %fusion.1, bf16[1,4096,384]{2,1,0:T(8,128)(2,1)S(1)} %copy-done, f32[32,384]{1,0:T(8,128)S(1)} %fusion.8, f32[32,384]{1,0:T(8,128)S(1)} %fusion.3), kind=kOutput, calls=%fused_computation.1 | convolution fusion | flops 100999168 | bytes 4030464 | tf_op jit(solution)/shard_map/dot_general | solution.py:56
  40.4 0.0 reduce-scatter.2.cloned.1.call-update
  40.4 0.7 copy.12
  41.1 4.9 %all-to-all-start.3 = ((bf16[32,4,1024]{2,0,1:T(8,128)(2,1)}), bf16[32,4,1024]{2,0,1:T(8,128)(2,1)S(1)}, u32[]{:S(2)}, u32[]{:S(2)}) async-start(bf16[32,4,1024]{2,0,1:T(8,128)(2,1)} %bitcast.29), calls=%async_computation.4 | async-start | bytes 524288 | tf_op jit(solution)/shard_map/all_to_all | solution.py:68
  46.0 0.0 copy-done.2
  46.1 15.7 %all_gather.7 = bf16[128,384]{1,0:T(8,128)(2,1)} all-gather(bf16[32,384]{1,0:T(8,128)(2,1)S(1)} %copy-done.2), channel_id=1, replica_groups=mesh['dp'=4,'expert'=4,'loop'=2] {'dp'}, dimensions={0}, use_global_device_ids=true | all-gather | bytes 122880 | tf_op jit(solution)/shard_map/all_gather | solution.py:69
  61.8 0.0 reduce-scatter.2.cloned.1.call-done
  61.8 1.6 %all_to_all.44 = bf16[4,4,4096]{2,1,0:T(4,128)(2,1)} reshape(bf16[16,4096]{1,0:T(8,128)(2,1)} %reduce-scatter.2.cloned.1.call-done) | data formatting | bytes 262144 | tf_op jit(solution)/shard_map/all_to_all | solution.py:67
  63.4 0.0 all-to-all-done.3
  63.4 3.3 %all-to-all-start.2 = ((bf16[4,4,4096]{2,1,0:T(4,128)(2,1)}), bf16[4,4,4096]{2,1,0:T(4,128)(2,1)S(1)}, u32[]{:S(2)}, u32[]{:S(2)}) async-start(bf16[4,4,4096]{2,1,0:T(4,128)(2,1)} %all_to_all.44), calls=%async_computation.3 | async-start | bytes 262144 | tf_op jit(solution)/shard_map/all_to_all | solution.py:67
  66.8 2.4 %convolution_bitcast_fusion = f32[1,1024,384]{2,1,0:T(8,128)} fusion(bf16[128,1024]{1,0:T(8,128)(2,1)S(1)} %bitcast.30, bf16[128,384]{1,0:T(8,128)(2,1)} %all_gather.7), kind=kOutput, calls=%fused_computation.11 | convolution fusion | flops 100663296 | bytes 1933312 | tf_op jit(solution)/shard_map/dot_general | solution.py:70
  69.2 2.1 %all-to-all-done.2 = bf16[4,4,4096]{2,1,0:T(4,128)(2,1)S(1)} async-done(((bf16[4,4,4096]{2,1,0:T(4,128)(2,1)}), bf16[4,4,4096]{2,1,0:T(4,128)(2,1)S(1)}, u32[]{:S(2)}, u32[]{:S(2)}) %all-to-all-start.2) | async-done | bytes 131104 | tf_op jit(solution)/shard_map/all_to_all | solution.py:67
  71.3 0.7 all_to_all.46
  (1 shorter events, 0.0 us)
Async XLA Ops:
  7.2 29.2 %copy-start = (bf16[1,4096,384]{2,1,0:T(8,128)(2,1)S(1)}, bf16[1,4096,384]{2,1,0:T(8,128)(2,1)}, u32[]{:S(2)}) copy-start(bf16[1,4096,384]{2,1,0:T(8,128)(2,1)} %param.10) | copy-start | bytes 9437188
  9.9 8.9 %all-to-all-start = ((bf16[4,4,4096]{2,1,0:T(4,128)(2,1)}), bf16[4,4,4096]{2,1,0:T(4,128)(2,1)S(1)}, u32[]{:S(2)}, u32[]{:S(2)}) async-start(bf16[4,4,4096]{2,1,0:T(4,128)(2,1)} %all_to_all.38), calls=%async_computation | async-start | bytes 262144 | tf_op jit(solution)/shard_map/all_to_all | solution.py:18
  18.8 10.8 %all-to-all-start.1 = ((bf16[4,4,4096]{2,1,0:T(4,128)(2,1)}), bf16[4,4,4096]{2,1,0:T(4,128)(2,1)}, u32[]{:S(2)}, u32[]{:S(2)}) async-start(bf16[4,4,4096]{2,1,0:T(4,128)(2,1)} %all_to_all.41), calls=%async_computation.1 | async-start | bytes 262144 | tf_op jit(solution)/shard_map/all_to_all | solution.py:17
  22.7 39.1 %reduce-scatter.2.cloned.1.call-start = ((), (), s32[]{:S(2)}) async-start(), calls=%async_computation.5 | async-start | bytes 393216 | tf_op jit(solution)/shard_map/reduce_scatter | solution.py:59
  30.5 5.3 %copy-start.1 = (bf16[1,4096,384]{2,1,0:T(8,128)(2,1)S(1)}, bf16[1,4096,384]{2,1,0:T(8,128)(2,1)}, u32[]{:S(2)}) copy-start(bf16[1,4096,384]{2,1,0:T(8,128)(2,1)} %param.9) | copy-start | bytes 9437188
  30.5 5.3 %collective-permute-start = (bf16[16,4096]{1,0:T(8,128)(2,1)S(1)}, bf16[16,4096]{1,0:T(8,128)(2,1)S(1)}, u32[]{:S(2)}, u32[]{:S(2)}) collective-permute-start(bf16[16,4096]{1,0:T(8,128)(2,1)S(1)} %all_to_all.43), channel_id=1, source_target_pairs={{0,1},{1,0},{2,3},{3,2},{4,5},{5,4},{6,7},{7,6},{8,9},{9,8},{10,11... | collective-permute-start | bytes 393224 | tf_op jit(solution)/shard_map/ppermute | solution.py:25
  38.6 7.4 %copy-start.2 = (bf16[32,384]{1,0:T(8,128)(2,1)S(1)}, bf16[32,384]{1,0:T(8,128)(2,1)}, u32[]{:S(2)}) copy-start(bf16[32,384]{1,0:T(8,128)(2,1)} %get-tuple-element.4) | copy-start | bytes 73732
  41.1 22.3 %all-to-all-start.3 = ((bf16[32,4,1024]{2,0,1:T(8,128)(2,1)}), bf16[32,4,1024]{2,0,1:T(8,128)(2,1)S(1)}, u32[]{:S(2)}, u32[]{:S(2)}) async-start(bf16[32,4,1024]{2,0,1:T(8,128)(2,1)} %bitcast.29), calls=%async_computation.4 | async-start | bytes 524288 | tf_op jit(solution)/shard_map/all_to_all | solution.py:68
  63.4 7.9 %all-to-all-start.2 = ((bf16[4,4,4096]{2,1,0:T(4,128)(2,1)}), bf16[4,4,4096]{2,1,0:T(4,128)(2,1)S(1)}, u32[]{:S(2)}, u32[]{:S(2)}) async-start(bf16[4,4,4096]{2,1,0:T(4,128)(2,1)} %all_to_all.44), calls=%async_computation.3 | async-start | bytes 262144 | tf_op jit(solution)/shard_map/all_to_all | solution.py:67
Sparse Core Ops, SparseCore 0:
  40.5 13.1 reduce-scatter.1
